TPU v7x, 32 devices: a whole 2x2x4 slice. The times are simulated.
32 devices in a mesh: groups: 2 (over x), frames: 16 (over z, y, core).
Axes of the slice: x: 2, y: 2, z: 4, core: 2. Of those that a mesh axis runs over, the one named last changes fastest.
Arguments:
- video: float32 [4, 16, 256, 256], P('groups', 'frames'), parts along dimension 0, may hold values from -9 to 9
- clip_start: int32 [4], P('groups'), parts along dimension 0, may hold values from 0 to 7
- gain_space: float32 [256], replicated, may hold values from 0.1 to 1.9
- qkv_space: float32 [256, 768], replicated, may hold values from -0.375 to 0.375
- out_space: float32 [256, 256], replicated, may hold values from -0.375 to 0.375
- gain_time: float32 [256], replicated, may hold values from 0.1 to 1.9
- qkv_time: float32 [256, 768], replicated, may hold values from -0.375 to 0.375
- out_time: float32 [256, 256], replicated, may hold values from -0.375 to 0.375
- code_sums: float32 [8192, 256], P(('groups', 'frames')), parts along dimension 0, may hold values from -12 to 12
- code_counts: float32 [8192], P(('groups', 'frames')), parts along dimension 0, may hold values from 1 to 10
Outputs:
- latents: float32 [4, 16, 256, 256], P('groups', None, 'frames'), parts along dimension 0
- new_sums: float32 [8192, 256], P(('groups', 'frames')), parts along dimension 0
- new_counts: float32 [8192], P(('groups', 'frames')), parts along dimension 0
- new_codebook: float32 [8192, 256], P(('groups', 'frames')), parts along dimension 0
There are 2 independent parts, one for each index of `groups`. A program takes and returns all parts, laid end to end along the dimension named above; an argument that names none is the same for every part. Nothing has to cross between parts.
All inputs are finite; a program needn't handle non-finite values.
Results may differ from a plain program's by a relative error of at most 0.0003.
Values sent between devices are 32-bit elements; how exact they have to be, the bound alone decides.
A program may use at most 64 MiB of HBM per device.

v0:
```python
import jax
import jax.numpy as jnp
from jax import lax
from jax.sharding import PartitionSpec as P

HEADS = 4


ATTN_SCALE = 10.0
SOFTMAX_WARMTH = 0.05
DECAY_RATE = 0.9
EPSILON = 1e-06
TOP_PRECISION = lax.Precision.HIGHEST


def rms_norm(values, gain_vec):
    return values * lax.rsqrt(jnp.mean(values * values, -1, keepdims=True) + EPSILON) * gain_vec


def unit_vec(values):
    return values * lax.rsqrt(jnp.sum(values * values, -1, keepdims=True) + EPSILON)


def spatial_block(one_frame, gain_vec, w_qkv, w_out):
    width = one_frame.shape[-1]
    normed = rms_norm(one_frame, gain_vec)
    packed = jnp.dot(normed, w_qkv, precision=TOP_PRECISION)
    queries = unit_vec(packed[:, :width].reshape(-1, HEADS, width // HEADS))
    key_vecs = unit_vec(packed[:, width : 2 * width].reshape(-1, HEADS, width // HEADS))
    values = packed[:, 2 * width :].reshape(-1, HEADS, width // HEADS)
    scores = ATTN_SCALE * jnp.einsum("qhd,khd->hqk", queries, key_vecs, precision=TOP_PRECISION)
    assignment_weights = jnp.exp(scores)
    totals = jnp.sum(assignment_weights, -1).T[:, :, None]
    mixed = jnp.einsum("hqk,khd->qhd", assignment_weights, values, precision=TOP_PRECISION) / totals
    return one_frame + jnp.dot(mixed.reshape(-1, width), w_out, precision=TOP_PRECISION)


def time_block(spaced, clip_start, gain_vec, w_qkv, w_out):
    clips, frames, places, width = spaced.shape
    normed = rms_norm(spaced, gain_vec)
    packed = jnp.einsum("ctpd,de->ctpe", normed, w_qkv, precision=TOP_PRECISION)
    shape_heads = (clips, frames, places, HEADS, width // HEADS)
    queries = unit_vec(packed[..., :width].reshape(shape_heads))
    key_vecs = unit_vec(packed[..., width : 2 * width].reshape(shape_heads))
    values = packed[..., 2 * width :].reshape(shape_heads)
    scores = ATTN_SCALE * jnp.einsum(
        "ctphd,csphd->cphts", queries, key_vecs, precision=TOP_PRECISION
    )
    later = jnp.arange(frames, dtype=jnp.int32)[:, None]
    earlier = jnp.arange(frames, dtype=jnp.int32)[None, :]
    allowed = (earlier <= later)[None] & (
        (earlier[None] >= clip_start[:, None, None]) | (earlier == later)[None]
    )
    assignment_weights = jnp.exp(scores) * allowed[:, None, None, :, :].astype(jnp.float32)
    totals = jnp.transpose(jnp.sum(assignment_weights, -1), (0, 3, 1, 2))[..., None]
    mixed = (
        jnp.einsum("cphts,csphd->ctphd", assignment_weights, values, precision=TOP_PRECISION)
        / totals
    )
    return spaced + jnp.einsum(
        "ctpd,de->ctpe", mixed.reshape(clips, frames, places, width), w_out, precision=TOP_PRECISION
    )


def local(
    video,
    clip_start,
    gain_space,
    qkv_space,
    out_space,
    gain_time,
    qkv_time,
    out_time,
    code_sums,
    code_counts,
):
    clips, local_frames, places, width = video.shape
    flat_frames = video.reshape(clips * local_frames, places, width)
    spaced = lax.map(
        lambda one_frame: spatial_block(one_frame, gain_space, qkv_space, out_space), flat_frames
    )
    spaced = spaced.reshape(clips, local_frames, places, width)
    by_place = lax.all_to_all(spaced, "frames", split_axis=2, concat_axis=1, tiled=True)
    latents = time_block(by_place, clip_start, gain_time, qkv_time, out_time)
    unit_token_vectors = unit_vec(latents.reshape(-1, width))
    local_codes = unit_vec(code_sums / code_counts[:, None])
    codebook_matrix = lax.all_gather(local_codes, "frames", axis=0, tiled=True)
    assignment_weights = jnp.exp(
        jnp.dot(unit_token_vectors, codebook_matrix.T, precision=TOP_PRECISION) / SOFTMAX_WARMTH
    )
    probs = assignment_weights / jnp.sum(assignment_weights, 1, keepdims=True)
    term_sums = lax.dot_general(
        probs, unit_token_vectors, (((0,), (0,)), ((), ())), precision=TOP_PRECISION
    )
    term_counts = jnp.sum(probs, 0)
    got_sums, got_counts = (
        lax.psum_scatter(term_sums, "frames", scatter_dimension=0, tiled=True),
        lax.psum_scatter(term_counts, "frames", scatter_dimension=0, tiled=True),
    )
    new_sums = DECAY_RATE * code_sums + (1.0 - DECAY_RATE) * got_sums
    new_counts = DECAY_RATE * code_counts + (1.0 - DECAY_RATE) * got_counts
    new_codebook = new_sums / new_counts[:, None]
    return (latents, new_sums, new_counts, new_codebook)


def solution(mesh):
    in_specs = (
        P("groups", "frames", None, None),
        P("groups"),
        P(),
        P(),
        P(),
        P(),
        P(),
        P(),
        P(("groups", "frames"), None),
        P(("groups", "frames")),
    )
    out_specs = (
        P("groups", None, "frames", None),
        P(("groups", "frames"), None),
        P(("groups", "frames")),
        P(("groups", "frames"), None),
    )
    return jax.shard_map(local, mesh=mesh, in_specs=in_specs, out_specs=out_specs, check_vma=False)
```

profile of v0, /device:TPU:8, one launch (start us, length us, event | category | flops | bytes accessed | tf_op | source)
XLA Modules:
  0.0 196.6 jit_solution(9034979632726046601)
XLA Ops:
  7.2 0.0 copy-start
  7.2 0.0 all-gather.2.cloned.1.call-start
  7.2 1.2 multiply_reduce_fusion.6
  8.4 1.8 broadcast_multiply_fusion.2
  10.2 0.0 all-gather.2.cloned.1.call-update
  10.3 0.0 copy-start.10
  10.3 0.0 copy-start.9
  10.3 25.9 %while.10 = (s32[]{:T(128)}, f32[2,256,256]{2,0,1:T(2,128)}, f32[2,256,256]{2,1,0:T(8,128)}, f32[256]{0:T(256)}, f32[256,768]{1,0:T(8,128)}, /*index=5*/f32[256,256]{1,0:T(8,128)}, s32[]{:T(128)}, s32[]{:T(128)}) while((s32[]{:T(128)}, f32[2,256,256]{2,0,1:T(2,128)}, f32[2,256,256]{2,1,0:T(8,128)}, f32[256]{0:T(256)}, f32[256,768]{1,0:T(8,128)}, ...), condition=%wide.region_5.6_spmd, body=%wide.region_0.5_spmd.sunk | while | flops 1209269504 | bytes 14202521 | solution.py:79
  10.3 1.1 fusion.67
  11.5 2.1 %fusion.68 = f32[256,768]{1,0:T(8,128)S(1)} fusion(f32[256,768]{1,0:T(8,128)} %get-tuple-element.142, f32[2,256,256]{2,1,0:T(8,128)} %get-tuple-element.140, s32[]{:T(128)} %get-tuple-element.130, f32[256]{0:T(256)} %get-tuple-element.141, f32[256]{0:T(256)S(1)} %add_rsqrt_fusion.10), kind=kOutput, calls=%fused_computation.10.clone.1 | convolution fusion | flops 604110848 | bytes 1837568 | tf_op jit(solution)/shard_map/while/body/eval_jaxpr/dot_general | solution.py:27
  13.6 0.1 fusion.69
  13.6 0.1 copy.84
  13.8 0.1 copy.83
  14.0 1.1 fusion.70
  15.1 0.1 copy.82
  15.3 0.8 fusion.71
  16.1 0.6 fusion.72
  16.7 0.3 copy.85
  16.9 6.3 %dynamic_update_slice.5 = f32[2,256,256]{2,0,1:T(2,128)} dynamic-update-slice(f32[2,256,256]{2,0,1:T(2,128)} %get-tuple-element.131, f32[1,256,256]{2,0,1:T(1,128)S(1)} %copy.85, s32[]{:T(128)} %get-tuple-element.130, s32[]{:T(128)} %constant.22.clone.1..sunk, s32[]{:T(128)} %constant.22.clone.1..sunk) | dynamic-update-slice | bytes 524292 | tf_op jit(solution)/shard_map/while/body/jit(dynamic_update_index_in_dim)/dynamic_update_slice | solution.py:79
  23.3 1.1 fusion.67
  24.4 2.1 %fusion.68 = f32[256,768]{1,0:T(8,128)S(1)} fusion(f32[256,768]{1,0:T(8,128)} %get-tuple-element.142, f32[2,256,256]{2,1,0:T(8,128)} %get-tuple-element.140, s32[]{:T(128)} %get-tuple-element.130, f32[256]{0:T(256)} %get-tuple-element.141, f32[256]{0:T(256)S(1)} %add_rsqrt_fusion.10), kind=kOutput, calls=%fused_computation.10.clone.1 | convolution fusion | flops 604110848 | bytes 1837568 | tf_op jit(solution)/shard_map/while/body/eval_jaxpr/dot_general | solution.py:27
  26.5 0.1 fusion.69
  26.6 0.1 copy.84
  26.7 0.1 copy.83
  26.9 1.1 fusion.70
  28.1 0.1 copy.82
  28.2 0.8 fusion.71
  29.0 0.6 fusion.72
  29.6 0.3 copy.85
  29.9 6.3 %dynamic_update_slice.5 = f32[2,256,256]{2,0,1:T(2,128)} dynamic-update-slice(f32[2,256,256]{2,0,1:T(2,128)} %get-tuple-element.131, f32[1,256,256]{2,0,1:T(1,128)S(1)} %copy.85, s32[]{:T(128)} %get-tuple-element.130, s32[]{:T(128)} %constant.22.clone.1..sunk, s32[]{:T(128)} %constant.22.clone.1..sunk) | dynamic-update-slice | bytes 524292 | tf_op jit(solution)/shard_map/while/body/jit(dynamic_update_index_in_dim)/dynamic_update_slice | solution.py:79
  36.2 6.3 %all-to-all-start = ((f32[2,1,256,256]{3,0,1,2:T(2,128)}), f32[2,1,256,256]{3,0,1,2:T(2,128)S(1)}, u32[]{:S(2)}, u32[]{:S(2)}) async-start(f32[2,1,256,256]{3,0,1,2:T(2,128)} %bitcast.103), calls=%async_computation | async-start | bytes 1048576 | tf_op jit(solution)/shard_map/all_to_all | solution.py:83
  42.5 0.0 reduce-scatter.2.cloned.1.call-start
  42.6 0.1 iota_compare_fusion.2
  42.6 0.1 and_convert_fusion
  42.7 25.3 %all-to-all-done = f32[2,1,256,256]{3,0,1,2:T(2,128)S(1)} async-done(((f32[2,1,256,256]{3,0,1,2:T(2,128)}), f32[2,1,256,256]{3,0,1,2:T(2,128)S(1)}, u32[]{:S(2)}, u32[]{:S(2)}) %all-to-all-start) | async-done | bytes 524320 | tf_op jit(solution)/shard_map/all_to_all | solution.py:83
  68.0 0.3 multiply_reduce_fusion.5
  68.4 0.1 copy.48
  68.6 0.1 copy.47
  68.7 1.5 fusion.23
  70.1 1.2 fusion.37
  71.3 0.5 reshape.172
  71.7 1.5 reshape.171
  73.2 2.5 %reshape.170 = f32[2,16,16,4,64]{4,3,2,1,0:T(4,128)} reshape(f32[2,16,16,256]{3,2,1,0:T(8,128)} %get-tuple-element.58) | data formatting | bytes 1048576 | tf_op jit(solution)/shard_map/reshape | solution.py:45
  75.7 0.6 multiply_reduce_fusion.2
  76.3 0.6 multiply_reduce_fusion.3
  77.0 1.5 broadcast_multiply_fusion
  78.5 3.1 %fusion.38 = (f32[2,16,4,16]{3,2,1,0:T(4,128)S(1)}, f32[2,16,4,16,16]{3,4,2,1,0:T(8,128)S(1)}) fusion(f32[2,16,16]{1,2,0:T(8,128)S(1)} %and_convert_fusion, f32[2,16,16,4,64]{4,3,2,1,0:T(4,128)S(1)} %get-tuple-element.69, f32[2,16,16,4,64]{4,3,2,1,0:T(4,128)S(1)} %get-tuple-element.70), kind=kOutput, calls=%fused_computation.72 | convolution fusion | flops 25262080 | bytes 1189888 | tf_op jit(solution)/shard_map/ctphd,csphd->cphts/dot_general | solution.py:46
  81.7 2.5 %fusion.17 = f32[2,16,16,4,64]{4,1,3,2,0:T(8,128)S(1)} fusion(f32[2,16,4,16,16]{3,4,2,1,0:T(8,128)S(1)} %get-tuple-element.62, f32[2,16,16,4,64]{4,3,2,1,0:T(4,128)S(1)} %copy-done.6, f32[2,16,16,4]{1,3,2,0:T(4,128)S(1)} %bitcast.106), kind=kOutput, calls=%fused_computation.28 | convolution fusion | flops 25296896 | bytes 1187840 | tf_op jit(solution)/shard_map/cphts,csphd->ctphd/dot_general | solution.py:57
  84.2 0.4 copy.53
  84.6 0.6 reshape.173
  85.2 1.6 multiply_reduce_fusion.4
  86.9 0.1 rsqrt.75
  87.0 0.1 bitcast_multiply_fusion.2
  87.1 0.0 all-gather.2.cloned.1.call-done
  87.1 9.9 %fusion.16 = (f32[512]{0:T(512)S(1)}, f32[512,4096]{1,0:T(8,128)S(1)}) fusion(f32[512,256]{1,0:T(8,128)S(1)} %bitcast_multiply_fusion.2, f32[4096,256]{1,0:T(8,128)} %all-gather.2.cloned.1.call-done), kind=kOutput, calls=%fused_computation.26 | convolution fusion | flops 6446644736 | bytes 13109248 | tf_op jit(solution)/shard_map/dot_general | solution.py:89
  97.1 3.2 %copy-done.1 = f32[512,4096]{1,0:T(8,128)} copy-done((f32[512,4096]{1,0:T(8,128)}, f32[512,4096]{1,0:T(8,128)S(1)}, u32[]{:S(2)}) %copy-start.1) | copy-done | bytes 8388632
  100.3 15.0 %fusion.28 = f32[4096,256]{1,0:T(8,128)} fusion(f32[512,256]{1,0:T(8,128)S(1)} %bitcast_multiply_fusion.2, f32[512,4096]{1,0:T(8,128)S(1)} %get-tuple-element.66, f32[512]{0:T(512)S(1)} %get-tuple-element.65), kind=kOutput, calls=%fused_computation.48 | convolution fusion | flops 6446645248 | bytes 13109248 | tf_op jit(solution)/shard_map/dot_general | solution.py:92
  115.3 0.0 reduce-scatter.2.cloned.1.call-update
  115.4 0.6 dynamic-slice
  116.6 4.3 %fusion.27 = f32[4096]{0:T(1024)S(1)} fusion(f32[512]{0:T(512)S(1)} %get-tuple-element.65, f32[512,4096]{1,0:T(8,128)} %copy-done.1), kind=kLoop, calls=%fused_computation.47 | loop fusion | flops 6287360 | bytes 8407040 | tf_op jit(solution)/shard_map/reduce_sum | solution.py:95
  120.9 53.5 %all-reduce = f32[4096]{0:T(1024)S(1)} all-reduce(f32[4096]{0:T(1024)S(1)} %fusion.27), channel_id=3, replica_groups=mesh['groups'=2,'frames'=16] {'frames'}, use_global_device_ids=true, to_apply=%region_15.16.clone | all-reduce | flops 4096 | bytes 32768
  174.3 0.1 fusion.33
  174.4 13.6 %reduce-scatter.2.cloned.1.call-done = f32[256,256]{1,0:T(8,128)} async-done(((f32[4096,256]{1,0:T(8,128)}), f32[256,256]{1,0:T(8,128)}) %reduce-scatter.2.cloned.1.call-update) | async-done | bytes 262160 | tf_op jit(solution)/shard_map/reduce_scatter | solution.py:97
  188.0 1.8 broadcast_divide_fusion
  (39 shorter events, 0.4 us)
Async XLA Ops:
  7.2 61.5 %copy-start = (f32[256,768]{1,0:T(8,128)S(1)}, f32[256,768]{1,0:T(8,128)}, u32[]{:S(2)}) copy-start(f32[256,768]{1,0:T(8,128)} %param.18) | copy-start | bytes 2359300
  7.2 79.9 %all-gather.2.cloned.1.call-start = ((), (), s32[]{:S(2)}) async-start(), calls=%async_computation.2 | async-start | bytes 4456448 | tf_op jit(solution)/shard_map/all_gather | solution.py:87
  10.3 32.3 %copy-start.10 = (s32[2]{0:T(128)S(1)}, s32[2]{0:T(128)}, u32[]{:S(2)}) copy-start(s32[2]{0:T(128)} %param.13) | copy-start | bytes 28
  10.3 58.4 %copy-start.9 = (f32[256]{0:T(256)S(1)}, f32[256]{0:T(256)}, u32[]{:S(2)}) copy-start(f32[256]{0:T(256)} %param.17) | copy-start | bytes 3076
  10.3 5.7 %copy-start.2 = (f32[2,256,256]{2,1,0:T(8,128)S(1)}, f32[2,256,256]{2,1,0:T(8,128)}, u32[]{:S(2)}) copy-start(f32[2,256,256]{2,1,0:T(8,128)} %get-tuple-element.140) | copy-start | bytes 1572868 | tf_op jit(solution)/shard_map/while
  10.3 5.7 %copy-start.3 = (f32[256,256]{1,0:T(8,128)S(1)}, f32[256,256]{1,0:T(8,128)}, u32[]{:S(2)}) copy-start(f32[256,256]{1,0:T(8,128)} %get-tuple-element.143) | copy-start | bytes 786436 | tf_op jit(solution)/shard_map/while
  23.3 5.7 %copy-start.2 = (f32[2,256,256]{2,1,0:T(8,128)S(1)}, f32[2,256,256]{2,1,0:T(8,128)}, u32[]{:S(2)}) copy-start(f32[2,256,256]{2,1,0:T(8,128)} %get-tuple-element.140) | copy-start | bytes 1572868 | tf_op jit(solution)/shard_map/while
  23.3 5.7 %copy-start.3 = (f32[256,256]{1,0:T(8,128)S(1)}, f32[256,256]{1,0:T(8,128)}, u32[]{:S(2)}) copy-start(f32[256,256]{1,0:T(8,128)} %get-tuple-element.143) | copy-start | bytes 786436 | tf_op jit(solution)/shard_map/while
  36.2 31.9 %all-to-all-start = ((f32[2,1,256,256]{3,0,1,2:T(2,128)}), f32[2,1,256,256]{3,0,1,2:T(2,128)S(1)}, u32[]{:S(2)}, u32[]{:S(2)}) async-start(f32[2,1,256,256]{3,0,1,2:T(2,128)} %bitcast.103), calls=%async_computation | async-start | bytes 1048576 | tf_op jit(solution)/shard_map/all_to_all | solution.py:83
  42.5 145.5 %reduce-scatter.2.cloned.1.call-start = ((), (), s32[]{:S(2)}) async-start(), calls=%async_computation.3 | async-start | bytes 4456448 | tf_op jit(solution)/shard_map/reduce_scatter | solution.py:97
  75.7 6.0 %copy-start.6 = (f32[2,16,16,4,64]{4,3,2,1,0:T(4,128)S(1)}, f32[2,16,16,4,64]{4,3,2,1,0:T(4,128)}, u32[]{:S(2)}) copy-start(f32[2,16,16,4,64]{4,3,2,1,0:T(4,128)} %reshape.170) | copy-start | bytes 1572868
  86.9 28.5 %copy-start.5 = (f32[2,16,16,256]{3,2,1,0:T(8,128)}, f32[2,16,16,256]{3,2,1,0:T(8,128)S(1)}, u32[]{:S(2)}) copy-start(f32[2,16,16,256]{3,2,1,0:T(8,128)S(1)} %get-tuple-element.64) | copy-start | bytes 1572868
  97.1 3.2 %copy-start.1 = (f32[512,4096]{1,0:T(8,128)}, f32[512,4096]{1,0:T(8,128)S(1)}, u32[]{:S(2)}) copy-start(f32[512,4096]{1,0:T(8,128)S(1)} %get-tuple-element.66) | copy-start | bytes 25165828
  100.3 15.1 %copy-start.11 = (u32[32]{0:T(128)S(1)}, u32[32]{0:T(128)}, u32[]{:S(2)}) copy-start(u32[32]{0:T(128)} %constant.46) | copy-start | bytes 388
  115.3 59.0 %copy-start.7 = (f32[256]{0:T(256)S(1)}, f32[256]{0:T(256)}, u32[]{:S(2)}) copy-start(f32[256]{0:T(256)} %param.21) | copy-start | bytes 3076
  115.3 72.6 %copy-start.4 = (f32[256,256]{1,0:T(8,128)S(1)}, f32[256,256]{1,0:T(8,128)}, u32[]{:S(2)}) copy-start(f32[256,256]{1,0:T(8,128)} %param.20) | copy-start | bytes 786436
  174.4 15.3 %copy-start.8 = (f32[256]{0:T(256)}, f32[256]{0:T(256)S(1)}, u32[]{:S(2)}) copy-start(f32[256]{0:T(256)S(1)} %fusion.33) | copy-start | bytes 3076
Sparse Core Ops, SparseCore 0:
  10.7 57.5 all-gather.1
  115.5 72.4 reduce-scatter.1
where the time goes:
time: 200 us; the launch traced here: 197 us
  blocking collectives  53.5 us (27%)
  matrix products  42.9 us (21%)
  waiting for transfers between devices  38.9 us (19%)
  local copies, waits for them, and re-layouts  24.8 us (12%)
  other arithmetic  15 us (8%)
  between operations  14.9 us (7%)
  starting transfers between devices  6.38 us (3%)
    unnamed x1, blocking collectives  53.5 us
    all_to_all x1, waiting for transfers between devices, local(): lax.all_to_all(spaced, 'frames', split_axis=2, concat_axis=1, tiled=True)  25.3 us
    dot_general x1, matrix products, local(): lax.dot_general(probs, unit_token_vectors, (((0,), (0,)), ((), ())), prec...  15 us
    reduce_scatter x1, waiting for transfers between devices, local(): lax.psum_scatter(term_sums, 'frames', scatter_dimension=0, tiled=True)  13.6 us
    dynamic_update_slice x4, local copies, waits for them, and re-layouts, local(): lax.map(lambda one_frame: spatial_block(one_frame, gain_space, qkv_space,...  13.2 us
    dot_general x1, matrix products, local(): jnp.dot(unit_token_vectors, codebook_matrix.T, precision=TOP_PRECISION)  9.91 us
    all_to_all x1, starting transfers between devices, local(): lax.all_to_all(spaced, 'frames', split_axis=2, concat_axis=1, tiled=True)  6.31 us
    reduce_sum x1, other arithmetic, local(): term_counts = jnp.sum(probs, 0)  4.27 us
  transfers between devices with their start and end apart: 3, of which 2 were waited for; matrix products, arithmetic and copies ran while one was open for 25% of the time, Pallas kernels for 0%

commit v1 on v0

v1 whole, which is shorter than its diff:
```python
import functools

import jax
import jax.numpy as jnp
from jax import lax
from jax.experimental import pallas as pl
from jax.experimental.pallas import tpu as pltpu
from jax.sharding import PartitionSpec as P

HEADS = 4
ATTN_SCALE = 10.0
SOFTMAX_WARMTH = 0.05
DECAY_RATE = 0.9
EPSILON = 1e-06
F32 = jnp.float32
BF16 = jnp.bfloat16
NN = (((1,), (0,)), ((), ()))
NT = (((1,), (1,)), ((), ()))


def split(a):
    hi = a.astype(BF16)
    return hi, (a - hi.astype(F32)).astype(BF16)


def dot(a, b, dims=NN):
    return lax.dot_general(a, b, dims, preferred_element_type=F32)


def dot3(a, b, dims=NN):
    return dot(a[0], b[0], dims) + (dot(a[0], b[1], dims) + dot(a[1], b[0], dims))


def dot2(a, b, dims=NN):
    return dot(a[0], b, dims) + dot(a[1], b, dims)


def attention(x, gain, w_qkv, w_out, mask):
    rows, width = x.shape
    hd = width // HEADS
    lane_i = lax.broadcasted_iota(jnp.int32, (width, width), 0) // hd
    lane_j = lax.broadcasted_iota(jnp.int32, (width, width), 1) // hd
    same_head = jnp.where(lane_i == lane_j, 1.0, 0.0).astype(BF16)
    row_head = lax.broadcasted_iota(jnp.int32, (rows, width), 1) // hd

    normed = x * lax.rsqrt(jnp.mean(x * x, -1, keepdims=True) + EPSILON) * gain
    packed = dot3(split(normed), w_qkv)
    q, k, v = packed[:, :width], packed[:, width : 2 * width], packed[:, 2 * width :]
    q = q * lax.rsqrt(dot2(split(q * q), same_head) + EPSILON) * ATTN_SCALE
    k = k * lax.rsqrt(dot2(split(k * k), same_head) + EPSILON)
    qh, ql = split(q)
    ks = split(k)
    vh, vl = split(v)
    mixed = None
    for h in range(HEADS):
        mine = jnp.where(row_head == h, 1.0, 0.0).astype(BF16)
        e = jnp.exp(dot3((qh * mine, ql * mine), ks, NT))
        if mask is not None:
            e = e * mask
        es = split(e)
        o = dot3(es, (vh * mine, vl * mine))
        t = dot2(es, mine)
        mixed, totals = (o, t) if h == 0 else (mixed + o, totals + t)
    return x + dot3(split(mixed / totals), w_out)


def body(
    n,
    video,
    starts,
    gain_space,
    qkv_space,
    out_space,
    gain_time,
    qkv_time,
    out_time,
    code_sums,
    code_counts,
    latents,
    new_sums,
    new_counts,
    new_codebook,
    spaced,
    xin,
    codes,
    weights,
    u_hi,
    u_lo,
    cs,
    ck,
    cr,
    ys,
    yr,
    zs,
    zr,
    a2a_send,
    a2a_recv,
    gz_send,
    gz_recv,
    gy_send,
    gy_recv,
    gc_send,
    gc_recv,
    rc_send,
    rc_recv,
    ry_send,
    ry_recv,
    rz_send,
    rz_recv,
):
    clips, places, width = video.shape
    share = places // n
    rows = code_sums.shape[0]
    n4 = n // 4
    halves = ck.shape[1]
    part = rows // halves
    tokens = clips * places

    me = lax.axis_index("frames")
    zz, b1, b0 = me // 4, (me // 2) % 2, me % 2
    y_mate = zz * 4 + (1 - b1) * 2 + b0
    c_mate = zz * 4 + b1 * 2 + (1 - b0)
    pending = []

    def remote(src, dst, ssem, rsem, dev):
        return pltpu.make_async_remote_copy(
            src_ref=src, dst_ref=dst, send_sem=ssem, recv_sem=rsem,
            device_id={"frames": dev}, device_id_type=pl.DeviceIdType.MESH,
        )

    def send(src, dst, ssem, rsem, dev):
        cp = remote(src, dst, ssem, rsem, dev)
        cp.start()
        pending.append(cp)

    barrier = pltpu.get_barrier_semaphore()

    def greet(i, c):
        pl.semaphore_signal(
            barrier, inc=1, device_id={"frames": lax.rem(me + i, n)},
            device_id_type=pl.DeviceIdType.MESH,
        )
        return c

    lax.fori_loop(1, n, greet, 0)

    own = code_sums[...] / jnp.transpose(jnp.broadcast_to(code_counts[...], (width, rows)))
    own = own * lax.rsqrt(jnp.sum(own * own, -1, keepdims=True) + EPSILON)
    codes[me] = own
    pl.semaphore_wait(barrier, n - 1)

    def block(d, y, c):
        return lax.rem(zz + d, n4) * 4 + y * 2 + c

    def back(d, y, c):
        return lax.rem(zz + n4 - d, n4) * 4 + y * 2 + c

    def gather_z(d):
        send(codes.at[me], codes.at[me], gz_send.at[d], gz_recv.at[d], block(d, b1, b0))

    def forward_own(d):
        g = back(d, b1, b0)
        if d:
            remote(codes.at[g], codes.at[g], gz_send.at[d], gz_recv.at[d], me).wait_recv()
        send(codes.at[g], codes.at[g], gy_send.at[d], gy_recv.at[d], y_mate)
        send(codes.at[g], codes.at[g], gc_send.at[d], gc_recv.at[d], c_mate)

    def forward_y(d):
        g = back(d, 1 - b1, b0)
        remote(codes.at[g], codes.at[g], gy_send.at[d], gy_recv.at[d], me).wait_recv()
        send(codes.at[g], codes.at[g], gc_send.at[n4 + d], gc_recv.at[n4 + d], c_mate)

    def arrived(d):
        for g, s in ((back(d, b1, 1 - b0), d), (back(d, 1 - b1, 1 - b0), n4 + d)):
            remote(codes.at[g], codes.at[g], gc_send.at[s], gc_recv.at[s], me).wait_recv()

    forward_own(0)
    if n4 > 1:
        gather_z(1)

    w_q, w_o = split(qkv_space[...]), split(out_space[...])
    gain = gain_space[...]
    for c in range(clips):
        spaced[c] = attention(video[c], gain, w_q, w_o, None)
        for d in range(1, n):
            to = lax.rem(me + d, n)
            send(
                spaced.at[c, pl.ds(pl.multiple_of(to * share, 8), share), :],
                xin.at[c, me], a2a_send.at[c, d], a2a_recv.at[c, d], to,
            )
        xin[c, me] = spaced[c, pl.ds(pl.multiple_of(me * share, 8), share), :]
    for d in range(2, n4):
        gather_z(d)

    w_q, w_o = split(qkv_time[...]), split(out_time[...])
    gain = gain_time[...]
    bits = share.bit_length() - 1
    r_i = lax.broadcasted_iota(jnp.int32, (places, places), 0)
    r_j = lax.broadcasted_iota(jnp.int32, (places, places), 1)
    t_i, t_j = r_i >> bits, r_j >> bits
    same_place = (r_i & (share - 1)) == (r_j & (share - 1))
    nxt = 1
    forwarded_y = 0
    for c in range(clips):
        if nxt < n4:
            forward_own(nxt)
            nxt += 1
            forward_y(forwarded_y)
            forwarded_y += 1
        for d in range(1, n):
            src = lax.rem(me + n - d, n)
            remote(xin.at[c, src], xin.at[c, src], a2a_send.at[c, d], a2a_recv.at[c, d], me).wait_recv()
        allowed = same_place & (t_j <= t_i) & ((t_j >= starts[c]) | (t_j == t_i))
        mask = jnp.where(allowed, 1.0, 0.0)
        y = attention(xin[c].reshape(places, width), gain, w_q, w_o, mask)
        latents[c] = y.reshape(n, share, width)
        u = y * lax.rsqrt(jnp.sum(y * y, -1, keepdims=True) + EPSILON)
        u_hi[0, pl.ds(c * places, places), :], u_lo[0, pl.ds(c * places, places), :] = split(u)
        u = u * (1.0 / SOFTMAX_WARMTH)
        u_hi[1, pl.ds(c * places, places), :], u_lo[1, pl.ds(c * places, places), :] = split(u)
    while nxt < n4:
        forward_own(nxt)
        nxt += 1
        forward_y(forwarded_y)
        forwarded_y += 1

    def score(g, acc):
        e = jnp.exp(dot3(split(codes[g]), (u_hi[1], u_lo[1]), NT))
        weights[g] = e
        return acc + jnp.sum(e.reshape(rows // 8, 8, tokens), 0)

    acc = jnp.zeros((8, tokens), F32)
    for d in range(n4):
        if forwarded_y <= d:
            forward_y(forwarded_y)
            forwarded_y += 1
        arrived(d)
        base = lax.rem(zz + n4 - d, n4) * 4
        acc = lax.fori_loop(0, 4, lambda i, a: score(base + i, a), acc)
    inv = 1.0 / jnp.sum(acc, 0, keepdims=True)
    ones = jnp.ones((8, tokens), BF16)

    def term(g, h, dst):
        ps = split(weights[g, pl.ds(h * part, part), :] * inv)
        dst[pl.ds(0, part), :] = dot3(ps, (u_hi[0], u_lo[0]))
        cnt = dot(ones, ps[0], NT) + dot(ones, ps[1], NT)
        if part < width:
            cnt = jnp.concatenate([cnt, jnp.zeros((8, width - part), F32)], 1)
        dst[pl.ds(part, 8), :] = cnt

    def start(d, h):
        for j in range(2):
            y = lax.rem(b1 + 1 + j, 2)
            term(block(d, y, 1 - b0), h, cs.at[d, h, j])
            send(cs.at[d, h, j], cr.at[d, h, j], rc_send.at[d, h, j], rc_recv.at[d, h, j], c_mate)
        for j in range(2):
            y = lax.rem(b1 + 1 + j, 2)
            term(block(d, y, b0), h, ck.at[d, h, j])

    def wait_core(d, h, j):
        remote(cr.at[d, h, j], cr.at[d, h, j], rc_send.at[d, h, j], rc_recv.at[d, h, j], me).wait_recv()

    def pair(d, h):
        wait_core(d, h, 0)
        ys[d, h] = ck[d, h, 0] + cr[d, h, 0]
        send(ys.at[d, h], yr.at[d, h], ry_send.at[d, h], ry_recv.at[d, h], y_mate)

    def across(d, h):
        wait_core(d, h, 1)
        remote(yr.at[d, h], yr.at[d, h], ry_send.at[d, h], ry_recv.at[d, h], me).wait_recv()
        zs[d, h] = ck[d, h, 1] + cr[d, h, 1] + yr[d, h]
        if d:
            send(zs.at[d, h], zr.at[d, h], rz_send.at[d, h], rz_recv.at[d, h], block(d, b1, b0))

    steps = [(d % n4, h) for d in range(1, n4 + 1) for h in range(halves)]
    total = len(steps)
    for i in range(total + 2):
        if i < total:
            start(*steps[i])
        if 1 <= i <= total:
            pair(*steps[i - 1])
        if i >= 2:
            across(*steps[i - 2])

    for h in range(halves):
        tot = zs[0, h]
        for d in range(1, n4):
            remote(zr.at[d, h], zr.at[d, h], rz_send.at[d, h], rz_recv.at[d, h], me).wait_recv()
            tot = tot + zr[d, h]
        span = pl.ds(h * part, part)
        sums = DECAY_RATE * code_sums[span, :] + (1.0 - DECAY_RATE) * tot[:part]
        counts = DECAY_RATE * code_counts[:, span] + (1.0 - DECAY_RATE) * tot[part : part + 1, :part]
        new_sums[span, :] = sums
        new_counts[:, span] = counts
        new_codebook[span, :] = sums / jnp.transpose(jnp.broadcast_to(counts, (width, part)))
    for cp in pending:
        cp.wait_send()


def local(n, video, clip_start, gain_space, qkv_space, out_space, gain_time, qkv_time, out_time, code_sums, code_counts):
    clips, _, places, width = video.shape
    rows = code_sums.shape[0]
    share, n4 = places // n, n // 4
    halves = 2 if rows >= 256 else 1
    high = rows // halves + 8
    tokens = clips * places
    vmem = pl.BlockSpec(memory_space=pltpu.VMEM)
    dma = pltpu.SemaphoreType.DMA
    lat, sums, counts, book = pl.pallas_call(
        functools.partial(body, n),
        out_shape=(
            jax.ShapeDtypeStruct((clips, n, share, width), F32),
            jax.ShapeDtypeStruct((rows, width), F32),
            jax.ShapeDtypeStruct((1, rows), F32),
            jax.ShapeDtypeStruct((rows, width), F32),
        ),
        in_specs=[vmem, pl.BlockSpec(memory_space=pltpu.SMEM)] + [vmem] * 8,
        out_specs=(vmem,) * 4,
        scratch_shapes=[
            pltpu.VMEM((clips, places, width), F32),
            pltpu.VMEM((clips, n, share, width), F32),
            pltpu.VMEM((n, rows, width), F32),
            pltpu.VMEM((n, rows, tokens), F32),
            pltpu.VMEM((2, tokens, width), BF16),
            pltpu.VMEM((2, tokens, width), BF16),
            pltpu.VMEM((n4, halves, 2, high, width), F32),
            pltpu.VMEM((n4, halves, 2, high, width), F32),
            pltpu.VMEM((n4, halves, 2, high, width), F32),
            pltpu.VMEM((n4, halves, high, width), F32),
            pltpu.VMEM((n4, halves, high, width), F32),
            pltpu.VMEM((n4, halves, high, width), F32),
            pltpu.VMEM((n4, halves, high, width), F32),
            dma((clips, n)), dma((clips, n)),
            dma((n4,)), dma((n4,)),
            dma((n4,)), dma((n4,)),
            dma((2 * n4,)), dma((2 * n4,)),
            dma((n4, halves, 2)), dma((n4, halves, 2)),
            dma((n4, halves)), dma((n4, halves)),
            dma((n4, halves)), dma((n4, halves)),
        ],
        compiler_params=pltpu.CompilerParams(
            collective_id=0, has_side_effects=True, vmem_limit_bytes=60 * 2**20
        ),
        name="tokenizer",
    )(
        video.reshape(clips, places, width), clip_start, gain_space.reshape(1, -1), qkv_space, out_space,
        gain_time.reshape(1, -1), qkv_time, out_time, code_sums, code_counts.reshape(1, -1),
    )
    return lat, sums, counts.reshape(rows), book


def solution(mesh):
    in_specs = (
        P("groups", "frames", None, None),
        P("groups"),
        P(),
        P(),
        P(),
        P(),
        P(),
        P(),
        P(("groups", "frames"), None),
        P(("groups", "frames")),
    )
    out_specs = (
        P("groups", None, "frames", None),
        P(("groups", "frames"), None),
        P(("groups", "frames")),
        P(("groups", "frames"), None),
    )
    fn = functools.partial(local, mesh.shape["frames"])
    return jax.shard_map(fn, mesh=mesh, in_specs=in_specs, out_specs=out_specs, check_vma=False)
```

time: 200 us -> 95.7 us (0.48); the launches traced: 197 us -> 95.5 us
  Pallas kernels: 0 us -> 91 us
  blocking collectives: 53.5 us -> 0 us
  matrix products: 42.9 us -> 0 us
  waiting for transfers between devices: 38.9 us -> 0 us
  local copies, waits for them, and re-layouts: 24.8 us -> 3.89 us
  other arithmetic: 15 us -> 0 us
  between operations: 14.9 us -> 0.66 us
  starting transfers between devices: 6.38 us -> 0 us
    pallas_call x0 -> x1, Pallas kernels: none -> 91 us  [local(): pl.pallas_call(functools.partial(body, n), out_shape=(jax.ShapeDtypeStruc...]
    unnamed x1 -> x0, blocking collectives: 53.5 us -> none
    dot_general x14 -> x0, matrix products: 42.9 us -> none  [the longest x1 15 us: local(): lax.dot_general(probs, unit_token_vectors, (((0,), (0,)), ((), ())), prec...]
    all_to_all x1 -> x0, waiting for transfers between devices: 25.3 us -> none  [local(): lax.all_to_all(spaced, 'frames', split_axis=2, concat_axis=1, tiled=True)]
    reduce_scatter x1 -> x0, waiting for transfers between devices: 13.6 us -> none  [local(): lax.psum_scatter(term_sums, 'frames', scatter_dimension=0, tiled=True)]
    dynamic_update_slice x4 -> x0, local copies, waits for them, and re-layouts: 13.2 us -> none  [local(): lax.map(lambda one_frame: spatial_block(one_frame, gain_space, qkv_space,...]
    reduce_sum x11 -> x0, other arithmetic: 9.44 us -> none  [the longest x1 4.27 us: local(): term_counts = jnp.sum(probs, 0)]
    all_to_all x1 -> x0, starting transfers between devices: 6.31 us -> none  [local(): lax.all_to_all(spaced, 'frames', split_axis=2, concat_axis=1, tiled=True)]
  transfers between devices with their start and end apart: 3 -> 0, of which waited for: 2 -> 0; matrix products, arithmetic and copies ran while one was open for 25% -> 0% of each run, Pallas kernels for 0% -> 0%
where the time goes in v1:
time: 95.7 us; the launch traced here: 95.5 us
  Pallas kernels  91 us (95%)
  local copies, waits for them, and re-layouts  3.89 us (4%)
    pallas_call x1, Pallas kernels, local(): pl.pallas_call(functools.partial(body, n), out_shape=(jax.ShapeDtypeStruc...  91 us
    unnamed x10, local copies, waits for them, and re-layouts  3.89 us

profile of v1, /device:TPU:8, one launch (start us, length us, event | category | flops | bytes accessed | tf_op | source)
XLA Modules:
  0.0 95.5 jit_solution(4580263660451129510)
XLA Ops:
  0.6 91.0 %tokenizer.1 = (f32[2,16,16,256]{3,2,1,0:T(8,128)}, f32[256,256]{1,0:T(8,128)}, f32[1,256]{1,0:T(1,128)}, f32[256,256]{1,0:T(8,128)}) custom-call(f32[2,256,256]{2,1,0:T(8,128)} %bitcast.5, s32[2]{0:T(128)} %starts.1, f32[1,256]{1,0:T(1,128)} %bitcast.6, f32[256,768]{1,0:T(8,128)} %qkv_space.1, f32[256,256]{1,0:T(8,128)} %out_space.1, f32[1,256]{1,0:T(1,128)} %bitcast.7, ...), custom_call_target="tpu_custom_call" | custom-call | tf_op jit(solution)/shard_map/tokenizer/pallas_call | solution.py:309
  91.6 0.0 copy-start.1
  91.6 1.9 %copy.18 = f32[2,16,16,256]{3,2,1,0:T(8,128)} copy(f32[2,16,16,256]{3,2,1,0:T(8,128)} %get-tuple-element.16) | data formatting | bytes 1048576
  93.5 0.0 copy-done.1
  93.5 0.0 copy-start.2
  93.5 0.0 copy-start
  93.5 0.7 copy.19
  94.2 0.0 copy-done.2
  94.2 0.6 copy.20
  94.8 0.0 copy-done
  94.8 0.7 copy.21
Async XLA Ops:
  91.6 1.9 %copy-start.1 = (f32[256,256]{1,0:T(8,128)S(1)}, f32[256,256]{1,0:T(8,128)}, u32[]{:S(2)}) copy-start(f32[256,256]{1,0:T(8,128)} %get-tuple-element.17) | copy-start | bytes 786436
  93.5 0.7 copy-start.2
  93.5 1.3 %copy-start = (f32[256,256]{1,0:T(8,128)S(1)}, f32[256,256]{1,0:T(8,128)}, u32[]{:S(2)}) copy-start(f32[256,256]{1,0:T(8,128)} %get-tuple-element.19) | copy-start | bytes 786436

commit v2 on v1

--- a/solution.py
+++ b/solution.py
@@ -77,9 +77,8 @@
     code_sums,
     code_counts,
     latents,
-    new_sums,
-    new_counts,
-    new_codebook,
+    terms,
+    acc,
     spaced,
     xin,
     codes,
@@ -152,31 +151,72 @@
     def block(d, y, c):
         return lax.rem(zz + d, n4) * 4 + y * 2 + c
 
-    def back(d, y, c):
-        return lax.rem(zz + n4 - d, n4) * 4 + y * 2 + c
-
-    def gather_z(d):
-        send(codes.at[me], codes.at[me], gz_send.at[d], gz_recv.at[d], block(d, b1, b0))
-
-    def forward_own(d):
-        g = back(d, b1, b0)
-        if d:
-            remote(codes.at[g], codes.at[g], gz_send.at[d], gz_recv.at[d], me).wait_recv()
-        send(codes.at[g], codes.at[g], gy_send.at[d], gy_recv.at[d], y_mate)
-        send(codes.at[g], codes.at[g], gc_send.at[d], gc_recv.at[d], c_mate)
-
-    def forward_y(d):
-        g = back(d, 1 - b1, b0)
-        remote(codes.at[g], codes.at[g], gy_send.at[d], gy_recv.at[d], me).wait_recv()
-        send(codes.at[g], codes.at[g], gc_send.at[n4 + d], gc_recv.at[n4 + d], c_mate)
-
-    def arrived(d):
-        for g, s in ((back(d, b1, 1 - b0), d), (back(d, 1 - b1, 1 - b0), n4 + d)):
-            remote(codes.at[g], codes.at[g], gc_send.at[s], gc_recv.at[s], me).wait_recv()
+    def reach(side, s):
+        at = zz - s if side == 0 else zz + s
+        return at, (at >= 0 if side == 0 else at < n4)
+
+    def slot(side, s):
+        return 0 if s == 0 else side * (n4 - 1) + s
+
+    def each(s, do):
+        if s == 0:
+            do(0, 0)
+        else:
+            for side in range(2):
+                pl.when(reach(side, s)[1])(functools.partial(do, side, s))
+
+    def copy_of(g, ssem, rsem, k, dev):
+        return remote(codes.at[g], codes.at[g], ssem.at[k], rsem.at[k], dev)
+
+    def own_block(side, s):
+        return reach(side, s)[0] * 4 + b1 * 2 + b0
+
+    def y_block(side, s):
+        return reach(side, s)[0] * 4 + (1 - b1) * 2 + b0
+
+    def along(side, s):
+        ahead, there = reach(1 - side, 1)
+        k = side * n4 + s + 1
+        return copy_of(own_block(side, s), gz_send, gz_recv, k, ahead * 4 + b1 * 2 + b0), there
+
+    def forward_own(s):
+        def do(side, s):
+            g = own_block(side, s)
+            if s:
+                copy_of(g, gz_send, gz_recv, side * n4 + s, me).wait_recv()
+            for sd in range(2) if s == 0 else (side,):
+                if s + 1 < n4:
+                    cp, there = along(sd, s)
+                    pl.when(there)(cp.start)
+            k = slot(side, s)
+            copy_of(g, gy_send, gy_recv, k, y_mate).start()
+            copy_of(g, gc_send, gc_recv, k, c_mate).start()
+
+        each(s, do)
+
+    def forward_y(s):
+        def do(side, s):
+            g, k = y_block(side, s), slot(side, s)
+            copy_of(g, gy_send, gy_recv, k, me).wait_recv()
+            copy_of(g, gc_send, gc_recv, 2 * n4 + k, c_mate).start()
+
+        each(s, do)
+
+    def gather_sent(s):
+        def do(side, s):
+            for sd in range(2) if s == 0 else (side,):
+                if s + 1 < n4:
+                    cp, there = along(sd, s)
+                    pl.when(there)(cp.wait_send)
+            g, k = own_block(side, s), slot(side, s)
+            copy_of(g, gy_send, gy_recv, k, y_mate).wait_send()
+            copy_of(g, gc_send, gc_recv, k, c_mate).wait_send()
+            g = y_block(side, s)
+            copy_of(g, gc_send, gc_recv, 2 * n4 + k, c_mate).wait_send()
+
+        each(s, do)
 
     forward_own(0)
-    if n4 > 1:
-        gather_z(1)
 
     w_q, w_o = split(qkv_space[...]), split(out_space[...])
     gain = gain_space[...]
@@ -189,8 +229,8 @@
                 xin.at[c, me], a2a_send.at[c, d], a2a_recv.at[c, d], to,
             )
         xin[c, me] = spaced[c, pl.ds(pl.multiple_of(me * share, 8), share), :]
-    for d in range(2, n4):
-        gather_z(d)
+    if n4 > 1:
+        forward_own(1)
 
     w_q, w_o = split(qkv_time[...]), split(out_time[...])
     gain = gain_time[...]
@@ -199,14 +239,9 @@
     r_j = lax.broadcasted_iota(jnp.int32, (places, places), 1)
     t_i, t_j = r_i >> bits, r_j >> bits
     same_place = (r_i & (share - 1)) == (r_j & (share - 1))
-    nxt = 1
-    forwarded_y = 0
     for c in range(clips):
-        if nxt < n4:
-            forward_own(nxt)
-            nxt += 1
-            forward_y(forwarded_y)
-            forwarded_y += 1
+        if c == 1:
+            forward_y(0)
         for d in range(1, n):
             src = lax.rem(me + n - d, n)
             remote(xin.at[c, src], xin.at[c, src], a2a_send.at[c, d], a2a_recv.at[c, d], me).wait_recv()
@@ -218,26 +253,36 @@
         u_hi[0, pl.ds(c * places, places), :], u_lo[0, pl.ds(c * places, places), :] = split(u)
         u = u * (1.0 / SOFTMAX_WARMTH)
         u_hi[1, pl.ds(c * places, places), :], u_lo[1, pl.ds(c * places, places), :] = split(u)
-    while nxt < n4:
-        forward_own(nxt)
-        nxt += 1
-        forward_y(forwarded_y)
-        forwarded_y += 1
-
-    def score(g, acc):
+    if clips == 1:
+        forward_y(0)
+
+    def score(g):
         e = jnp.exp(dot3(split(codes[g]), (u_hi[1], u_lo[1]), NT))
         weights[g] = e
-        return acc + jnp.sum(e.reshape(rows // 8, 8, tokens), 0)
-
-    acc = jnp.zeros((8, tokens), F32)
-    for d in range(n4):
-        if forwarded_y <= d:
-            forward_y(forwarded_y)
-            forwarded_y += 1
-        arrived(d)
-        base = lax.rem(zz + n4 - d, n4) * 4
-        acc = lax.fori_loop(0, 4, lambda i, a: score(base + i, a), acc)
-    inv = 1.0 / jnp.sum(acc, 0, keepdims=True)
+        acc[...] += jnp.sum(e.reshape(rows // 8, 8, tokens), 0)
+
+    def score_all(s):
+        def do(side, s):
+            at, k = reach(side, s)[0], slot(side, s)
+            for y, k in ((b1, k), (1 - b1, 2 * n4 + k)):
+                copy_of(at * 4 + y * 2 + (1 - b0), gc_send, gc_recv, k, me).wait_recv()
+
+            def one(i, carry):
+                score(at * 4 + i)
+                return carry
+
+            lax.fori_loop(0, 4, one, 0)
+
+        each(s, do)
+
+    acc[...] = jnp.zeros((8, tokens), F32)
+    for s in range(2, n4 + 2):
+        if s < n4:
+            forward_own(s)
+        if s - 1 < n4:
+            forward_y(s - 1)
+        score_all(s - 2)
+    inv = 1.0 / jnp.sum(acc[...], 0, keepdims=True)
     ones = jnp.ones((8, tokens), BF16)
 
     def term(g, h, dst):
@@ -287,14 +332,25 @@
         for d in range(1, n4):
             remote(zr.at[d, h], zr.at[d, h], rz_send.at[d, h], rz_recv.at[d, h], me).wait_recv()
             tot = tot + zr[d, h]
+        terms[h] = tot
+    for s in range(n4):
+        gather_sent(s)
+    for cp in pending:
+        cp.wait_send()
+
+
+def finish(found, terms, code_sums, code_counts, latents, new_sums, new_counts, new_codebook):
+    halves, high, width = terms.shape
+    part = high - 8
+    latents[...] = found[...]
+    for h in range(halves):
+        tot = terms[h]
         span = pl.ds(h * part, part)
         sums = DECAY_RATE * code_sums[span, :] + (1.0 - DECAY_RATE) * tot[:part]
         counts = DECAY_RATE * code_counts[:, span] + (1.0 - DECAY_RATE) * tot[part : part + 1, :part]
         new_sums[span, :] = sums
         new_counts[:, span] = counts
         new_codebook[span, :] = sums / jnp.transpose(jnp.broadcast_to(counts, (width, part)))
-    for cp in pending:
-        cp.wait_send()
 
 
 def local(n, video, clip_start, gain_space, qkv_space, out_space, gain_time, qkv_time, out_time, code_sums, code_counts):
@@ -306,17 +362,16 @@
     tokens = clips * places
     vmem = pl.BlockSpec(memory_space=pltpu.VMEM)
     dma = pltpu.SemaphoreType.DMA
-    lat, sums, counts, book = pl.pallas_call(
+    found, terms = pl.pallas_call(
         functools.partial(body, n),
         out_shape=(
             jax.ShapeDtypeStruct((clips, n, share, width), F32),
-            jax.ShapeDtypeStruct((rows, width), F32),
-            jax.ShapeDtypeStruct((1, rows), F32),
-            jax.ShapeDtypeStruct((rows, width), F32),
+            jax.ShapeDtypeStruct((halves, high, width), F32),
         ),
         in_specs=[vmem, pl.BlockSpec(memory_space=pltpu.SMEM)] + [vmem] * 8,
-        out_specs=(vmem,) * 4,
+        out_specs=(vmem,) * 2,
         scratch_shapes=[
+            pltpu.VMEM((8, tokens), F32),
             pltpu.VMEM((clips, places, width), F32),
             pltpu.VMEM((clips, n, share, width), F32),
             pltpu.VMEM((n, rows, width), F32),
@@ -331,9 +386,9 @@
             pltpu.VMEM((n4, halves, high, width), F32),
             pltpu.VMEM((n4, halves, high, width), F32),
             dma((clips, n)), dma((clips, n)),
-            dma((n4,)), dma((n4,)),
-            dma((n4,)), dma((n4,)),
             dma((2 * n4,)), dma((2 * n4,)),
+            dma((2 * n4,)), dma((2 * n4,)),
+            dma((4 * n4,)), dma((4 * n4,)),
             dma((n4, halves, 2)), dma((n4, halves, 2)),
             dma((n4, halves)), dma((n4, halves)),
             dma((n4, halves)), dma((n4, halves)),
@@ -346,6 +401,18 @@
         video.reshape(clips, places, width), clip_start, gain_space.reshape(1, -1), qkv_space, out_space,
         gain_time.reshape(1, -1), qkv_time, out_time, code_sums, code_counts.reshape(1, -1),
     )
+    lat, sums, counts, book = pl.pallas_call(
+        finish,
+        out_shape=(
+            jax.ShapeDtypeStruct((clips, n, share, width), F32),
+            jax.ShapeDtypeStruct((rows, width), F32),
+            jax.ShapeDtypeStruct((1, rows), F32),
+            jax.ShapeDtypeStruct((rows, width), F32),
+        ),
+        in_specs=[vmem] * 4,
+        out_specs=(vmem,) * 4,
+        name="finish",
+    )(found, terms, code_sums, code_counts.reshape(1, -1))
     return lat, sums, counts.reshape(rows), book
 
 

time: 95.7 us -> 84.9 us (0.89)
  Pallas kernels: 91 us -> 84.1 us
  local copies, waits for them, and re-layouts: 3.89 us -> 0 us
    pallas_call x1, Pallas kernels: 91 us -> 81.9 us  [local(): pl.pallas_call(functools.partial(body, n), out_shape=(jax.ShapeDtypeStruc...]
    unnamed x10 -> x0, local copies, waits for them, and re-layouts: 3.89 us -> none
    pallas_call x0 -> x1, Pallas kernels: none -> 2.21 us  [local(): pl.pallas_call(finish, out_shape=(jax.ShapeDtypeStruct((clips, n, share,...]
where the time goes in v2:
time: 84.9 us; the launch traced here: 84.7 us
  Pallas kernels  84.1 us (99%)
    pallas_call x1, Pallas kernels, local(): pl.pallas_call(functools.partial(body, n), out_shape=(jax.ShapeDtypeStruc...  81.9 us
    pallas_call x1, Pallas kernels, local(): pl.pallas_call(finish, out_shape=(jax.ShapeDtypeStruct((clips, n, share,...  2.21 us

profile of v2, /device:TPU:8, one launch (start us, length us, event | category | flops | bytes accessed | tf_op | source)
XLA Modules:
  0.0 84.7 jit_solution(10850424458391860356)
XLA Ops:
  0.6 81.9 %tokenizer.1 = (f32[2,16,16,256]{3,2,1,0:T(8,128)}, f32[2,136,256]{2,1,0:T(8,128)}) custom-call(f32[2,256,256]{2,1,0:T(8,128)} %bitcast.5, s32[2]{0:T(128)} %starts.1, f32[1,256]{1,0:T(1,128)} %bitcast.8, f32[256,768]{1,0:T(8,128)} %qkv_space.1, f32[256,256]{1,0:T(8,128)} %out_space.1, f32[1,256]{1,0:T(1,128)} %bitcast.9, f32[256,768]{1,0:T(8,128)} %qkv_time.1, ...), custom_call_target="tpu_custom_call" | custom-call | tf_op jit(solution)/shard_map/tokenizer/pallas_call | solution.py:365
  82.5 2.2 %finish.1 = (f32[2,16,16,256]{3,2,1,0:T(8,128)}, f32[256,256]{1,0:T(8,128)}, f32[1,256]{1,0:T(1,128)}, f32[256,256]{1,0:T(8,128)}) custom-call(f32[2,16,16,256]{3,2,1,0:T(8,128)} %get-tuple-element.10.found, f32[2,136,256]{2,1,0:T(8,128)} %get-tuple-element.11.terms, f32[256,256]{1,0:T(8,128)} %code_sums.3, f32[1,256]{1,0:T(1,128)} %bitcast.7), custom_call_target="tpu_custom_call" | custom-call | tf_op jit(solution)/shard_map/finish/pallas_call | solution.py:404

commit v3 on v2

--- a/solution.py
+++ b/solution.py
@@ -322,8 +322,7 @@
     for i in range(total + 2):
         if i < total:
             start(*steps[i])
-        if 1 <= i <= total:
-            pair(*steps[i - 1])
+            pair(*steps[i])
         if i >= 2:
             across(*steps[i - 2])
 

time: 84.9 us -> 85.6 us (level)
  no operation moved by 1% of the time
where the time goes in v3:
time: 85.6 us; the launch traced here: 85.2 us
  Pallas kernels  84.6 us (99%)
    pallas_call x1, Pallas kernels, local(): pl.pallas_call(functools.partial(body, n), out_shape=(jax.ShapeDtypeStruc...  82.4 us
    pallas_call x1, Pallas kernels, local(): pl.pallas_call(finish, out_shape=(jax.ShapeDtypeStruct((clips, n, share,...  2.21 us

profile of v3, /device:TPU:8, one launch (start us, length us, event | category | flops | bytes accessed | tf_op | source)
XLA Modules:
  0.0 85.2 jit_solution(4428493739310804482)
XLA Ops:
  0.6 82.4 %tokenizer.1 = (f32[2,16,16,256]{3,2,1,0:T(8,128)}, f32[2,136,256]{2,1,0:T(8,128)}) custom-call(f32[2,256,256]{2,1,0:T(8,128)} %bitcast.5, s32[2]{0:T(128)} %starts.1, f32[1,256]{1,0:T(1,128)} %bitcast.8, f32[256,768]{1,0:T(8,128)} %qkv_space.1, f32[256,256]{1,0:T(8,128)} %out_space.1, f32[1,256]{1,0:T(1,128)} %bitcast.9, f32[256,768]{1,0:T(8,128)} %qkv_time.1, ...), custom_call_target="tpu_custom_call" | custom-call | tf_op jit(solution)/shard_map/tokenizer/pallas_call | solution.py:364
  83.0 2.2 %finish.1 = (f32[2,16,16,256]{3,2,1,0:T(8,128)}, f32[256,256]{1,0:T(8,128)}, f32[1,256]{1,0:T(1,128)}, f32[256,256]{1,0:T(8,128)}) custom-call(f32[2,16,16,256]{3,2,1,0:T(8,128)} %get-tuple-element.10.found, f32[2,136,256]{2,1,0:T(8,128)} %get-tuple-element.11.terms, f32[256,256]{1,0:T(8,128)} %code_sums.3, f32[1,256]{1,0:T(1,128)} %bitcast.7), custom_call_target="tpu_custom_call" | custom-call | tf_op jit(solution)/shard_map/finish/pallas_call | solution.py:403
